TPU v7x, 32 devices: a whole 2x2x4 slice. The times are simulated.
32 devices in a mesh: member: 8 (over z, core), dp: 4 (over y, x).
Axes of the slice: x: 2, y: 2, z: 4, core: 2. Of those that a mesh axis runs over, the one named last changes fastest.
Arguments:
- feats: bfloat16 [8, 2048, 1024], P('member', 'dp'), may hold values from -160 to 160
- pair_weight: float32 [8, 3], replicated, may hold values from 0.5 to 2
Outputs:
- grad_centred: float32 [8, 2048, 1024], P('member', 'dp')
- cka: float32 [8, 3], P('member')
All inputs are finite; a program needn't handle non-finite values.
Results may differ from a plain program's by a relative error of at most 0.0053.
Values may be sent and summed in bfloat16 or wider, within the bound.
A program may use at most 128 MiB of HBM per device.

v0:
```python
import math

import jax
import jax.numpy as jnp
from jax import lax
from jax.sharding import PartitionSpec as P


def passed_along(value, axis, steps):
    count = lax.axis_size(axis)
    pairs = [(source, (source + steps) % count) for source in range(count)]
    return lax.ppermute(value, axis, pairs)


def shards(feats, pair_weight):
    rows = feats[0]
    batch = rows.shape[0] * lax.axis_size("dp")
    members = lax.axis_size("member")
    pairs = pair_weight.shape[1]
    totals = lax.psum(jnp.sum(rows.astype(jnp.float32), axis=0), "dp")
    centred = (rows.astype(jnp.float32) - totals / batch).astype(jnp.bfloat16)
    partners = []
    for offset in range(1, pairs + 1):
        partners.append(passed_along(centred, "member", -offset))
    stacked = jnp.stack([centred] + partners)
    piece = lax.all_gather(stacked, "dp", axis=1, tiled=True)
    covs = jnp.einsum("rf,krg->kfg", piece[0], piece, preferred_element_type=jnp.float32)
    self_hsic = jnp.sum(covs[0] * covs[0])
    pair_hsic = jnp.sum(covs[1:] * covs[1:], axis=(1, 2))
    all_self, all_pair = (
        lax.all_gather(self_hsic[None], "member", axis=0, tiled=True),
        lax.all_gather(pair_hsic[None], "member", axis=0, tiled=True),
    )
    partner_self = jnp.stack([jnp.roll(all_self, -o) for o in range(1, pairs + 1)], axis=1)
    norms = jnp.sqrt(all_self[:, None] * partner_self)
    cka_all = all_pair / norms
    weighted = pair_weight * cka_all
    incoming = jnp.stack([jnp.roll(weighted[:, o - 1], o) for o in range(1, pairs + 1)], axis=1)
    member = lax.axis_index("member")
    chosen = (jnp.arange(members, dtype=jnp.int32) == member).astype(jnp.float32)[:, None]
    own_cka = jnp.sum(chosen * cka_all, axis=0)
    own_coef = jnp.sum(chosen * (2.0 * pair_weight / norms), axis=0)
    self_coef = (jnp.sum(chosen * weighted) + jnp.sum(chosen * incoming)) / (self_hsic + 1e-06)
    mixers = jnp.transpose((own_coef[:, None, None] * covs[1:]).astype(jnp.bfloat16), (1, 0, 2))
    self_mix = (2.0 * self_coef * covs[0]).astype(jnp.bfloat16)
    local = jnp.einsum("krg,fkg->rf", stacked[1:], mixers, preferred_element_type=jnp.float32)
    local = local - jnp.dot(centred, self_mix, preferred_element_type=jnp.float32)
    outgoing = jnp.einsum("rf,fkg->krg", centred, mixers, preferred_element_type=jnp.float32)
    returned = jnp.zeros_like(local)
    for offset in range(1, pairs + 1):
        returned = returned + passed_along(outgoing[offset - 1], "member", offset)
    grad = math.sqrt(batch) * (local + returned)
    return (grad[None], own_cka[None])


def solution(mesh):
    return jax.shard_map(
        shards,
        mesh=mesh,
        in_specs=(P("member", "dp", None), P()),
        out_specs=(P("member", "dp", None), P("member", None)),
        check_vma=False,
    )
```

profile of v0, /device:TPU:0, one launch (start us, length us, event | category | flops | bytes accessed | tf_op | source)
XLA Modules:
  0.0 468.1 jit_solution(16581469566564601588)
XLA Ops:
  7.2 1.4 convert_reduce_fusion
  8.6 11.4 %psum.7 = f32[1024]{0:T(1024)S(1)} all-reduce(f32[1024]{0:T(1024)S(1)} %convert_reduce_fusion), channel_id=1, replica_groups=mesh['member'=8,'dp'=4] {'dp'}, use_global_device_ids=true, to_apply=%region_1.0 | all-reduce | flops 1024 | bytes 8192 | tf_op jit(solution)/shard_map/psum | solution.py:20
  20.0 1.5 fusion.8
  21.5 1.1 collective-permute-start
  22.6 2.6 collective-permute-start.1
  25.2 1.5 fusion.9
  26.7 17.4 %collective-permute-done = bf16[512,1024]{1,0:T(8,128)(2,1)S(1)} collective-permute-done((bf16[512,1024]{1,0:T(8,128)(2,1)S(1)}, bf16[512,1024]{1,0:T(8,128)(2,1)S(1)}, u32[]{:S(2)}, u32[]{:S(2)}) %collective-permute-start) | collective-permute-done | bytes 1048608 | tf_op jit(solution)/shard_map/ppermute | solution.py:12
  44.0 25.5 %collective-permute-done.1 = bf16[512,1024]{1,0:T(8,128)(2,1)S(1)} collective-permute-done((bf16[512,1024]{1,0:T(8,128)(2,1)S(1)}, bf16[512,1024]{1,0:T(8,128)(2,1)S(1)}, u32[]{:S(2)}, u32[]{:S(2)}) %collective-permute-start.1) | collective-permute-done | bytes 1048608 | tf_op jit(solution)/shard_map/ppermute | solution.py:12
  69.6 10.3 %collective-permute-done.2 = bf16[512,1024]{1,0:T(8,128)(2,1)S(1)} collective-permute-done((bf16[512,1024]{1,0:T(8,128)(2,1)S(1)}, bf16[512,1024]{1,0:T(8,128)(2,1)S(1)}, u32[]{:S(2)}, u32[]{:S(2)}) %collective-permute-start.2) | collective-permute-done | bytes 1048608 | tf_op jit(solution)/shard_map/ppermute | solution.py:12
  80.8 2.2 pad_maximum_fusion
  85.0 166.4 %all-gather.3.cloned.1.call-done = bf16[4,2048,1024]{2,1,0:T(8,128)(2,1)} async-done(((bf16[4,512,1024]{2,1,0:T(8,128)(2,1)}), bf16[4,2048,1024]{2,1,0:T(8,128)(2,1)}) %all-gather.3.cloned.1.call-update) | async-done | bytes 16777232 | tf_op jit(solution)/shard_map/all_gather | solution.py:26
  251.4 22.4 %convolution_bitcast_fusion = f32[4,1024,1024]{1,2,0:T(8,128)S(1)} fusion(bf16[4,2048,1024]{2,1,0:T(8,128)(2,1)} %all-gather.3.cloned.1.call-done), kind=kOutput, calls=%fused_computation.2 | convolution fusion | flops 17179869184 | bytes 37748736 | tf_op jit(solution)/shard_map/rf,krg->kfg/dot_general | solution.py:27
  273.8 2.1 multiply_reduce_fusion.1
  275.9 1.6 multiply_reduce_fusion
  277.6 2.1 copy-done
  279.6 1.4 dynamic-update-slice
  281.2 16.2 %all-reduce.2 = (f32[24]{0:T(128)S(1)}, f32[8]{0:T(128)S(1)}) all-reduce(f32[24]{0:T(128)S(1)} %dynamic-update-slice.1, f32[8]{0:T(128)S(1)} %dynamic-update-slice), channel_id=2, replica_groups=mesh['member'=8,'dp'=4] {'member'}, use_global_device_ids=true, to_apply=%add.1 | all-reduce | flops 32 | bytes 256
  300.2 6.6 %convolution_bitcast_fusion.1 = f32[3,512,1024]{2,1,0:T(8,128)S(1)} fusion(bf16[512,1024]{1,0:T(8,128)(2,1)S(1)} %fusion.8, f32[4,1024,1024]{1,2,0:T(8,128)} %copy-done, f32[3]{0:T(128)S(1)} %get-tuple-element.5), kind=kOutput, calls=%fused_computation.17 | convolution fusion | flops 3227516928 | bytes 19922956 | tf_op jit(solution)/shard_map/rf,fkg->krg/dot_general | solution.py:48
  306.9 3.0 slice_bitcast_fusion.3
  312.2 3.6 fusion.11
  315.8 43.6 %collective-permute-done.3 = f32[512,1024]{1,0:T(8,128)} collective-permute-done((f32[512,1024]{1,0:T(8,128)}, f32[512,1024]{1,0:T(8,128)}, u32[]{:S(2)}, u32[]{:S(2)}) %collective-permute-start.3) | collective-permute-done | bytes 2097184 | tf_op jit(solution)/shard_map/ppermute | solution.py:12
  359.4 1.3 collective-permute-done.4
  360.7 89.2 %collective-permute-done.5 = f32[512,1024]{1,0:T(8,128)} collective-permute-done((f32[512,1024]{1,0:T(8,128)}, f32[512,1024]{1,0:T(8,128)}, u32[]{:S(2)}, u32[]{:S(2)}) %collective-permute-start.5) | collective-permute-done | bytes 2097184 | tf_op jit(solution)/shard_map/ppermute | solution.py:12
  449.8 11.4 %fusion.15 = f32[1,512,1024]{2,1,0:T(8,128)} fusion(f32[512,1024]{1,0:T(8,128)S(1)} %fusion.11, f32[512,1024]{1,0:T(8,128)} %collective-permute-done.5, f32[512,1024]{1,0:T(8,128)} %collective-permute-done.3, f32[512,1024]{1,0:T(8,128)} %collective-permute-done.4, bf16[1,512,1024]{2,1,0:T(8,128)(2,1)S(1)} %bitcast.82, ...), kind=kOutput, calls=%fused_computation.29 | convolution fusion | flops 3233284096 | bytes 26214412 | tf_op jit(solution)/shard_map/krg,fkg->rf/dot_general | solution.py:46
  (47 shorter events, 5.6 us)
Async XLA Ops:
  7.2 244.2 %all-gather.3.cloned.1.call-start = ((), (), s32[]{:S(2)}) async-start(), calls=%async_computation | async-start | bytes 20971520 | tf_op jit(solution)/shard_map/all_gather | solution.py:26
  21.5 22.5 %collective-permute-start = (bf16[512,1024]{1,0:T(8,128)(2,1)S(1)}, bf16[512,1024]{1,0:T(8,128)(2,1)S(1)}, u32[]{:S(2)}, u32[]{:S(2)}) collective-permute-start(bf16[512,1024]{1,0:T(8,128)(2,1)S(1)} %fusion.8), channel_id=1, source_target_pairs={{0,28},{4,0},{8,4},{12,8},{16,12},{20,16},{24,20},{28,24},{1,29},{... | collective-permute-start | bytes 3145736 | tf_op jit(solution)/shard_map/ppermute | solution.py:12
  22.6 47.0 %collective-permute-start.1 = (bf16[512,1024]{1,0:T(8,128)(2,1)S(1)}, bf16[512,1024]{1,0:T(8,128)(2,1)S(1)}, u32[]{:S(2)}, u32[]{:S(2)}) collective-permute-start(bf16[512,1024]{1,0:T(8,128)(2,1)S(1)} %fusion.8), channel_id=1, source_target_pairs={{0,24},{4,28},{8,0},{12,4},{16,8},{20,12},{24,16},{28,20},{1,25},{... | collective-permute-start | bytes 3145736 | tf_op jit(solution)/shard_map/ppermute | solution.py:12
  25.2 54.7 %collective-permute-start.2 = (bf16[512,1024]{1,0:T(8,128)(2,1)S(1)}, bf16[512,1024]{1,0:T(8,128)(2,1)S(1)}, u32[]{:S(2)}, u32[]{:S(2)}) collective-permute-start(bf16[512,1024]{1,0:T(8,128)(2,1)S(1)} %fusion.8), channel_id=1, source_target_pairs={{0,20},{4,24},{8,28},{12,0},{16,4},{20,8},{24,12},{28,16},{1,21},{... | collective-permute-start | bytes 3145736 | tf_op jit(solution)/shard_map/ppermute | solution.py:12
  44.0 35.8 %copy-start.1 = (bf16[512,1024]{1,0:T(8,128)(2,1)}, bf16[512,1024]{1,0:T(8,128)(2,1)S(1)}, u32[]{:S(2)}) copy-start(bf16[512,1024]{1,0:T(8,128)(2,1)S(1)} %collective-permute-done) | copy-start | bytes 3145732
  69.6 10.3 %copy-start.3 = (bf16[512,1024]{1,0:T(8,128)(2,1)}, bf16[512,1024]{1,0:T(8,128)(2,1)S(1)}, u32[]{:S(2)}) copy-start(bf16[512,1024]{1,0:T(8,128)(2,1)S(1)} %collective-permute-done.1) | copy-start | bytes 3145732
  79.9 1.0 copy-start.5
  83.1 0.7 copy-start.8
  273.8 5.8 %copy-start = (f32[4,1024,1024]{1,2,0:T(8,128)}, f32[4,1024,1024]{1,2,0:T(8,128)S(1)}, u32[]{:S(2)}) copy-start(f32[4,1024,1024]{1,2,0:T(8,128)S(1)} %convolution_bitcast_fusion) | copy-start | bytes 50331652
  275.9 22.0 %copy-start.7 = (f32[8,3]{0,1:T(4,128)S(1)}, f32[8,3]{0,1:T(4,128)}, u32[]{:S(2)}) copy-start(f32[8,3]{0,1:T(4,128)} %param.3) | copy-start | bytes 292
  309.9 139.9 %copy-start.2 = (bf16[512,1024]{1,0:T(8,128)(2,1)S(1)}, bf16[512,1024]{1,0:T(8,128)(2,1)}, u32[]{:S(2)}) copy-start(bf16[512,1024]{1,0:T(8,128)(2,1)} %copy-done.1) | copy-start | bytes 3145732
  309.9 139.9 %copy-start.4 = (bf16[512,1024]{1,0:T(8,128)(2,1)S(1)}, bf16[512,1024]{1,0:T(8,128)(2,1)}, u32[]{:S(2)}) copy-start(bf16[512,1024]{1,0:T(8,128)(2,1)} %copy-done.3) | copy-start | bytes 3145732
  309.9 49.5 %collective-permute-start.3 = (f32[512,1024]{1,0:T(8,128)}, f32[512,1024]{1,0:T(8,128)}, u32[]{:S(2)}, u32[]{:S(2)}) collective-permute-start(f32[512,1024]{1,0:T(8,128)} %get-tuple-element.12), channel_id=1, source_target_pairs={{0,4},{4,8},{8,12},{12,16},{16,20},{20,24},{24,28},{28,0},{1,5},{5... | collective-permute-start | bytes 6291464 | tf_op jit(solution)/shard_map/ppermute | solution.py:12
  309.9 50.8 %collective-permute-start.4 = (f32[512,1024]{1,0:T(8,128)}, f32[512,1024]{1,0:T(8,128)}, u32[]{:S(2)}, u32[]{:S(2)}) collective-permute-start(f32[512,1024]{1,0:T(8,128)} %get-tuple-element.10), channel_id=1, source_target_pairs={{0,8},{4,12},{8,16},{12,20},{16,24},{20,28},{24,0},{28,4},{1,9},{5... | collective-permute-start | bytes 6291464 | tf_op jit(solution)/shard_map/ppermute | solution.py:12
  309.9 139.9 %collective-permute-start.5 = (f32[512,1024]{1,0:T(8,128)}, f32[512,1024]{1,0:T(8,128)}, u32[]{:S(2)}, u32[]{:S(2)}) collective-permute-start(f32[512,1024]{1,0:T(8,128)} %get-tuple-element.11), channel_id=1, source_target_pairs={{0,12},{4,16},{8,20},{12,24},{16,28},{20,0},{24,4},{28,8},{1,13},{... | collective-permute-start | bytes 6291464 | tf_op jit(solution)/shard_map/ppermute | solution.py:12
  312.2 137.6 %copy-start.6 = (bf16[512,1024]{1,0:T(8,128)(2,1)S(1)}, bf16[512,1024]{1,0:T(8,128)(2,1)}, u32[]{:S(2)}) copy-start(bf16[512,1024]{1,0:T(8,128)(2,1)} %copy-done.5) | copy-start | bytes 3145732
Sparse Core Ops, SparseCore 0:
  83.2 168.1 all-gather.2
where the time goes:
time: 468 us
  waiting for transfers between devices  354 us (76%)
  matrix products  44 us (9%)
  blocking collectives  27.6 us (6%)
  between operations  16.8 us (4%)
  other arithmetic  12 us (3%)
  local copies, waits for them, and re-layouts  9.99 us (2%)
    ppermute x6, waiting for transfers between devices, passed_along(): return lax.ppermute(value, axis, pairs)  187 us
    all_gather x1, waiting for transfers between devices, shards(): piece = lax.all_gather(stacked, 'dp', axis=1, tiled=True)  166 us
    dot_general x1, matrix products, shards(): jnp.einsum('rf,krg->kfg', piece[0], piece, preferred_element_type=jnp.flo...  22.4 us
    unnamed x1, blocking collectives  16.2 us
    dot_general x1, matrix products, shards(): jnp.einsum('krg,fkg->rf', stacked[1:], mixers, preferred_element_type=jnp...  11.4 us
    psum x1, blocking collectives, shards(): totals = lax.psum(jnp.sum(rows.astype(jnp.float32), axis=0), 'dp')  11.4 us
  transfers between devices with their start and end apart: 7, of which 7 were waited for; matrix products, arithmetic and copies ran while one was open for 1% of the time, Pallas kernels for 0%

commit v1 on v0

v1 whole, which is shorter than its diff:
```python
import math

import jax
import jax.numpy as jnp
from jax import lax
from jax.sharding import PartitionSpec as P


def mixing(self_hsic, pair_hsic, pair_weight):
    pairs = pair_weight.shape[1]
    members = pair_weight.shape[0]
    partner_self = jnp.stack([jnp.roll(self_hsic, -o) for o in range(1, pairs + 1)], axis=1)
    norms = jnp.sqrt(self_hsic[:, None] * partner_self)
    cka = pair_hsic / norms
    weighted = pair_weight * cka
    incoming = sum(jnp.roll(weighted[:, o - 1], o) for o in range(1, pairs + 1))
    self_coef = (jnp.sum(weighted, axis=1) + incoming) / (self_hsic + 1e-06)
    coef = 2.0 * pair_weight / norms
    eye = jnp.eye(members, dtype=jnp.float32)
    mix = -2.0 * self_coef[:, None] * eye
    for o in range(1, pairs + 1):
        ahead = coef[:, o - 1][:, None] * jnp.roll(eye, o, axis=1)
        mix = mix + ahead + ahead.T
    return cka, mix


def shards(feats, pair_weight):
    rows = feats[0]
    members = lax.axis_size("member")
    pairs = pair_weight.shape[1]
    whole = lax.all_gather(rows, "dp", axis=0, tiled=True)
    batch, width = whole.shape
    mean = jnp.sum(whole.astype(jnp.float32), axis=0) / batch
    centred = (whole.astype(jnp.float32) - mean).astype(jnp.bfloat16)
    own = (rows.astype(jnp.float32) - mean).astype(jnp.bfloat16)
    blocks = centred.reshape(members, batch // members, width)
    gram = jnp.einsum("rf,mcf->mrc", own, blocks, preferred_element_type=jnp.float32)
    held = lax.all_to_all(gram.astype(jnp.bfloat16), "member", 0, 0)
    held = held.astype(jnp.float32)
    sums = []
    for o in range(pairs + 1):
        sums.append(jnp.sum(held * jnp.roll(held, -o, axis=0), axis=(1, 2)))
    sums = lax.psum(jnp.stack(sums, axis=1), ("member", "dp"))
    cka, mix = mixing(sums[:, 0], sums[:, 1:], pair_weight)
    mixed = jnp.stack(
        [sum(mix[m, q] * held[q] for q in range(members)) for m in range(members)]
    ).astype(jnp.bfloat16)
    mixed = lax.all_to_all(mixed, "member", 0, 0)
    grad = jnp.einsum("jrc,jcf->rf", mixed, blocks, preferred_element_type=jnp.float32)
    grad = math.sqrt(batch) * grad
    own_cka = lax.dynamic_slice_in_dim(cka, lax.axis_index("member"), 1, axis=0)
    return (grad[None], own_cka)


def solution(mesh):
    return jax.shard_map(
        shards,
        mesh=mesh,
        in_specs=(P("member", "dp", None), P()),
        out_specs=(P("member", "dp", None), P("member", None)),
        check_vma=False,
    )
```

time: 468 us -> 293 us (0.63)
  waiting for transfers between devices: 354 us -> 155 us
  other arithmetic: 12 us -> 58.2 us
  matrix products: 44 us -> 9.6 us
  blocking collectives: 27.6 us -> 37 us
  starting transfers between devices: 4.06 us -> 8.86 us
    ppermute x6 -> x0, waiting for transfers between devices: 187 us -> none  [passed_along(): return lax.ppermute(value, axis, pairs)]
    all_gather x1, waiting for transfers between devices: 166 us -> 57.2 us  [shards(): whole = lax.all_gather(rows, 'dp', axis=0, tiled=True)]
    all_to_all x0 -> x2, waiting for transfers between devices: none -> 97 us  [the longest x1 48.6 us: shards(): held = lax.all_to_all(gram.astype(jnp.bfloat16), 'member', 0, 0)]
    unnamed x0 -> x7, other arithmetic: none -> 43.5 us
    dot_general x4 -> x2, matrix products: 44 us -> 9.6 us  [the longest x1 5.85 us: shards(): jnp.einsum('jrc,jcf->rf', mixed, blocks, preferred_element_type=jnp.float32)]
    psum x1, blocking collectives: 11.4 us -> 37 us  [shards(): sums = lax.psum(jnp.stack(sums, axis=1), ('member', 'dp'))]
    unnamed x1 -> x0, blocking collectives: 16.2 us -> none
    all_to_all x0 -> x2, starting transfers between devices: none -> 8.82 us  [the longest x1 4.6 us: shards(): held = lax.all_to_all(gram.astype(jnp.bfloat16), 'member', 0, 0)]
  transfers between devices with their start and end apart: 7 -> 3, of which waited for: 7 -> 3; matrix products, arithmetic and copies ran while one was open for 1% -> 0% of each run, Pallas kernels for 0% -> 0%
where the time goes in v1:
time: 293 us; the launch traced here: 292 us
  waiting for transfers between devices  155 us (53%)
  other arithmetic  58.2 us (20%)
  blocking collectives  37 us (13%)
  between operations  14.1 us (5%)
  local copies, waits for them, and re-layouts  9.6 us (3%)
  matrix products  9.6 us (3%)
  starting transfers between devices  8.86 us (3%)
    all_gather x1, waiting for transfers between devices, shards(): whole = lax.all_gather(rows, 'dp', axis=0, tiled=True)  57.2 us
    all_to_all x1, waiting for transfers between devices, shards(): held = lax.all_to_all(gram.astype(jnp.bfloat16), 'member', 0, 0)  48.6 us
    all_to_all x1, waiting for transfers between devices, shards(): mixed = lax.all_to_all(mixed, 'member', 0, 0)  48.4 us
    unnamed x7, other arithmetic  43.5 us
    psum x1, blocking collectives, shards(): sums = lax.psum(jnp.stack(sums, axis=1), ('member', 'dp'))  37 us
    another operation x1, other arithmetic, shards(): jnp.stack([sum((mix[m, q] * held[q] for q in range(members))) for m in ra...  6.23 us
  transfers between devices with their start and end apart: 3, of which 3 were waited for; matrix products, arithmetic and copies ran while one was open for 0% of the time, Pallas kernels for 0%

profile of v1, /device:TPU:0, one launch (start us, length us, event | category | flops | bytes accessed | tf_op | source)
XLA Modules:
  0.0 292.4 jit_solution(5384150362921916437)
XLA Ops:
  7.9 57.2 %all-gather.3.cloned.1.call-done = bf16[1,2048,1024]{2,1,0:T(8,128)(2,1)} async-done(((bf16[1,512,1024]{2,1,0:T(8,128)(2,1)}), bf16[1,2048,1024]{2,1,0:T(8,128)(2,1)}) %all-gather.3.cloned.1.call-update) | async-done | bytes 4194320 | tf_op jit(solution)/shard_map/all_gather | solution.py:31
  65.1 3.0 %convert_reduce_fusion = f32[1024]{0:T(1024)S(1)} fusion(bf16[1,2048,1024]{2,1,0:T(8,128)(2,1)} %all-gather.3.cloned.1.call-done), kind=kLoop, calls=%fused_computation | loop fusion | flops 4193280 | bytes 4198400 | tf_op jit(solution)/shard_map/reduce_sum | solution.py:33
  68.6 1.3 fusion.1
  69.9 1.9 copy-done
  71.8 3.8 %convert_bitcast_fusion.1 = bf16[8,512,256]{1,2,0:T(8,128)(2,1)} fusion(bf16[8,256,1024]{2,1,0:T(8,128)(2,1)S(1)} %bitcast.136, bf16[1,512,1024]{2,1,0:T(8,128)(2,1)S(1)} %copy-done.2, f32[1024]{0:T(1024)S(1)} %broadcast_multiply_fusion), kind=kOutput, calls=%fused_computation.13 | convolution fusion | flops 2150105088 | bytes 7344128 | tf_op jit(solution)/shard_map/rf,mcf->mrc/dot_general | solution.py:37
  75.5 4.6 %all-to-all-start = ((bf16[8,512,256]{1,2,0:T(8,128)(2,1)}), bf16[8,512,256]{1,2,0:T(8,128)(2,1)S(1)}, u32[]{:S(2)}, u32[]{:S(2)}) async-start(bf16[8,512,256]{1,2,0:T(8,128)(2,1)} %convert_bitcast_fusion.1), calls=%async_computation | async-start | bytes 4194304 | tf_op jit(solution)/shard_map/all_to_all | solution.py:38
  80.5 48.6 %all-to-all-done = bf16[8,512,256]{1,2,0:T(8,128)(2,1)S(1)} async-done(((bf16[8,512,256]{1,2,0:T(8,128)(2,1)}), bf16[8,512,256]{1,2,0:T(8,128)(2,1)S(1)}, u32[]{:S(2)}, u32[]{:S(2)}) %all-to-all-start) | async-done | bytes 2097184 | tf_op jit(solution)/shard_map/all_to_all | solution.py:38
  130.9 1.8 multiply_reduce_fusion
  132.8 37.0 %psum.7 = f32[8,4]{0,1:T(4,128)S(1)} all-reduce(f32[8,4]{0,1:T(4,128)S(1)} %pad_maximum_fusion), channel_id=1, replica_groups=mesh['member'=8,'dp'=4] {'member','dp'}, use_global_device_ids=true, to_apply=%region_5.6 | all-reduce | flops 32 | bytes 256 | tf_op jit(solution)/shard_map/psum | solution.py:43
  170.5 0.7 maximum_bitcast_fusion
  172.2 0.7 slice_bitcast_fusion.1
  173.3 0.7 fusion.26
  175.4 0.7 fusion.24
  176.7 6.4 %fusion.9 = bf16[8,512,256]{1,2,0:T(8,128)(2,1)} fusion(f32[8,512,256]{1,2,0:T(8,128)S(1)} %convert_element_type.47, f32[]{:T(128)} %bitcast.34, f32[]{:T(128)} %bitcast.33, f32[]{:T(128)} %bitcast.32, f32[]{:T(128)} %bitcast.31, f32[]{:T(128)} %bitcast.30, f32[]{:T(128)} %bitcast.29, f32[]{:T(128)} %bitcast.28, f32[]{:T(128)} %bitcast.27), kind=kLoop, calls=%fused_computation.25 | loop fusion | flops 2097151 | bytes 4456480
  183.1 6.1 %fusion.10 = bf16[8,512,256]{1,2,0:T(8,128)(2,1)} fusion(bf16[8,512,256]{1,2,0:T(8,128)(2,1)} %fusion.9, f32[8,512,256]{1,2,0:T(8,128)S(1)} %convert_element_type.47, f32[]{:T(128)} %bitcast.42, f32[]{:T(128)} %bitcast.41, f32[]{:T(128)} %bitcast.40, f32[]{:T(128)} %bitcast.39, f32[]{:T(128)} %bitcast.38, f32[]{:T(128)} %bitcast.37, f32[]{:T(128)} %bitcast.36, ...), kind=kLoop, calls=%fused_computation.26 | loop fusion | flops 2097152 | bytes 4460544
  189.2 6.1 %fusion.11 = bf16[8,512,256]{1,2,0:T(8,128)(2,1)} fusion(bf16[8,512,256]{1,2,0:T(8,128)(2,1)} %fusion.10, f32[8,512,256]{1,2,0:T(8,128)S(1)} %convert_element_type.47, f32[]{:T(128)} %bitcast.50, f32[]{:T(128)} %bitcast.49, f32[]{:T(128)} %bitcast.48, f32[]{:T(128)} %bitcast.47, f32[]{:T(128)} %bitcast.46, f32[]{:T(128)} %bitcast.45, f32[]{:T(128)} %bitcast.44, ...), kind=kLoop, calls=%fused_computation.27 | loop fusion | flops 2097152 | bytes 4460544
  195.3 6.1 %fusion.12 = bf16[8,512,256]{1,2,0:T(8,128)(2,1)} fusion(bf16[8,512,256]{1,2,0:T(8,128)(2,1)} %fusion.11, f32[8,512,256]{1,2,0:T(8,128)S(1)} %convert_element_type.47, f32[]{:T(128)} %bitcast.58, f32[]{:T(128)} %bitcast.57, f32[]{:T(128)} %bitcast.56, f32[]{:T(128)} %bitcast.55, f32[]{:T(128)} %bitcast.54, f32[]{:T(128)} %bitcast.53, f32[]{:T(128)} %bitcast.52, ...), kind=kLoop, calls=%fused_computation.28 | loop fusion | flops 2097152 | bytes 4460544
  201.4 6.3 %fusion.13 = bf16[8,512,256]{1,2,0:T(8,128)(2,1)} fusion(bf16[8,512,256]{1,2,0:T(8,128)(2,1)} %fusion.12, f32[8,512,256]{1,2,0:T(8,128)S(1)} %convert_element_type.47, f32[]{:T(128)} %bitcast.66, f32[]{:T(128)} %bitcast.65, f32[]{:T(128)} %bitcast.64, f32[]{:T(128)} %bitcast.63, f32[]{:T(128)} %bitcast.62, f32[]{:T(128)} %bitcast.61, f32[]{:T(128)} %bitcast.60, ...), kind=kLoop, calls=%fused_computation.29 | loop fusion | flops 2097152 | bytes 4460544
  207.7 6.2 %fusion.14 = bf16[8,512,256]{1,2,0:T(8,128)(2,1)} fusion(bf16[8,512,256]{1,2,0:T(8,128)(2,1)} %fusion.13, f32[8,512,256]{1,2,0:T(8,128)S(1)} %convert_element_type.47, f32[]{:T(128)} %bitcast.74, f32[]{:T(128)} %bitcast.73, f32[]{:T(128)} %bitcast.72, f32[]{:T(128)} %bitcast.71, f32[]{:T(128)} %bitcast.70, f32[]{:T(128)} %bitcast.69, f32[]{:T(128)} %bitcast.68, ...), kind=kLoop, calls=%fused_computation.30 | loop fusion | flops 2097152 | bytes 4460544
  214.0 6.2 %fusion.15 = bf16[8,512,256]{1,2,0:T(8,128)(2,1)} fusion(bf16[8,512,256]{1,2,0:T(8,128)(2,1)} %fusion.14, f32[8,512,256]{1,2,0:T(8,128)S(1)} %convert_element_type.47, f32[]{:T(128)} %bitcast.82, f32[]{:T(128)} %bitcast.81, f32[]{:T(128)} %bitcast.80, f32[]{:T(128)} %bitcast.79, f32[]{:T(128)} %bitcast.78, f32[]{:T(128)} %bitcast.77, f32[]{:T(128)} %bitcast.76, ...), kind=kLoop, calls=%fused_computation.31 | loop fusion | flops 2097152 | bytes 4460544
  220.2 6.2 %fusion.16 = bf16[8,512,256]{1,2,0:T(8,128)(2,1)} fusion(bf16[8,512,256]{1,2,0:T(8,128)(2,1)} %fusion.15, f32[8,512,256]{1,2,0:T(8,128)S(1)} %convert_element_type.47, f32[]{:T(128)} %bitcast.90, f32[]{:T(128)} %bitcast.89, f32[]{:T(128)} %bitcast.88, f32[]{:T(128)} %bitcast.87, f32[]{:T(128)} %bitcast.86, f32[]{:T(128)} %bitcast.85, f32[]{:T(128)} %bitcast.84, ...), kind=kLoop, calls=%fused_computation.32 | loop fusion | flops 2097152 | bytes 4460544 | tf_op jit(solution)/shard_map/stack | solution.py:45
  226.4 4.2 %all-to-all-start.1 = ((bf16[8,512,256]{1,2,0:T(8,128)(2,1)}), bf16[8,512,256]{1,2,0:T(8,128)(2,1)S(1)}, u32[]{:S(2)}, u32[]{:S(2)}) async-start(bf16[8,512,256]{1,2,0:T(8,128)(2,1)} %fusion.16), calls=%async_computation.1 | async-start | bytes 4194304 | tf_op jit(solution)/shard_map/all_to_all | solution.py:48
  231.3 48.4 %all-to-all-done.1 = bf16[8,512,256]{1,2,0:T(8,128)(2,1)S(1)} async-done(((bf16[8,512,256]{1,2,0:T(8,128)(2,1)}), bf16[8,512,256]{1,2,0:T(8,128)(2,1)S(1)}, u32[]{:S(2)}, u32[]{:S(2)}) %all-to-all-start.1) | async-done | bytes 2097184 | tf_op jit(solution)/shard_map/all_to_all | solution.py:48
  279.7 5.9 %fusion.5 = f32[1,512,1024]{2,1,0:T(8,128)} fusion(bf16[8,512,256]{1,2,0:T(8,128)(2,1)S(1)} %all-to-all-done.1, bf16[8,256,1024]{2,1,0:T(8,128)(2,1)} %bitcast.137), kind=kOutput, calls=%fused_computation.12 | convolution fusion | flops 2148007936 | bytes 8388608 | tf_op jit(solution)/shard_map/jrc,jcf->rf/dot_general | solution.py:49
  (53 shorter events, 8.0 us)
Async XLA Ops:
  7.2 58.0 %all-gather.3.cloned.1.call-start = ((), (), s32[]{:S(2)}) async-start(), calls=%async_computation.2 | async-start | bytes 5242880 | tf_op jit(solution)/shard_map/all_gather | solution.py:31
  65.1 3.4 %copy-start.1 = (bf16[1,2048,1024]{2,1,0:T(8,128)(2,1)S(1)}, bf16[1,2048,1024]{2,1,0:T(8,128)(2,1)}, u32[]{:S(2)}) copy-start(bf16[1,2048,1024]{2,1,0:T(8,128)(2,1)} %all-gather.3.cloned.1.call-done) | copy-start | bytes 12582916
  68.6 3.2 %copy-start.2 = (bf16[1,512,1024]{2,1,0:T(8,128)(2,1)S(1)}, bf16[1,512,1024]{2,1,0:T(8,128)(2,1)}, u32[]{:S(2)}) copy-start(bf16[1,512,1024]{2,1,0:T(8,128)(2,1)} %param.2) | copy-start | bytes 3145732
  69.9 1.9 copy-start
  75.5 53.6 %all-to-all-start = ((bf16[8,512,256]{1,2,0:T(8,128)(2,1)}), bf16[8,512,256]{1,2,0:T(8,128)(2,1)S(1)}, u32[]{:S(2)}, u32[]{:S(2)}) async-start(bf16[8,512,256]{1,2,0:T(8,128)(2,1)} %convert_bitcast_fusion.1), calls=%async_computation | async-start | bytes 4194304 | tf_op jit(solution)/shard_map/all_to_all | solution.py:38
  130.9 40.5 %copy-start.3 = (f32[8,3]{0,1:T(4,128)S(1)}, f32[8,3]{0,1:T(4,128)}, u32[]{:S(2)}) copy-start(f32[8,3]{0,1:T(4,128)} %param.3) | copy-start | bytes 292
  226.4 53.3 %all-to-all-start.1 = ((bf16[8,512,256]{1,2,0:T(8,128)(2,1)}), bf16[8,512,256]{1,2,0:T(8,128)(2,1)S(1)}, u32[]{:S(2)}, u32[]{:S(2)}) async-start(bf16[8,512,256]{1,2,0:T(8,128)(2,1)} %fusion.16), calls=%async_computation.1 | async-start | bytes 4194304 | tf_op jit(solution)/shard_map/all_to_all | solution.py:48
Sparse Core Ops, SparseCore 0:
  9.8 55.2 all-gather.2

commit v2 on v1

v2 whole, which is shorter than its diff:
```python
import functools
import math

import jax
import jax.numpy as jnp
from jax import lax
from jax.experimental import pallas as pl
from jax.experimental.pallas import tpu as pltpu
from jax.sharding import PartitionSpec as P

MESH = pl.DeviceIdType.MESH
LANES = 128


def flipped(index, bits, count):
    place, value = 1, 0
    while place < count:
        bit = (index // place) % 2
        value = value + ((1 - bit) if bits & place else bit) * place
        place *= 2
    return value


def rolled(value, steps):
    count = value.shape[0]
    steps %= count
    if steps == 0:
        return value
    return jnp.concatenate([value[count - steps:], value[:count - steps]], axis=0)


def kernel(members, parts, pairs, x_ref, weight_ref, grad_ref, cka_ref, sums, raw, cent, gram, held,
           mixed, back, acc, stage, coefs, sum_send, sum_recv, raw_send, raw_recv, gram_send,
           gram_recv, back_send, back_recv, acc_send, acc_recv):
    me, mine = lax.axis_index("member"), lax.axis_index("dp")
    rows, width = x_ref.shape
    piece = rows // members
    half = rows // 2
    batch = rows * parts

    def across(t):
        return {"member": me, "dp": flipped(mine, t, parts)}

    def along(i):
        return {"member": lax.rem(me + i, members), "dp": mine}

    def source(i):
        return lax.rem(me + members - i, members)

    def remote(src, dst, send, recv, to):
        return pltpu.make_async_remote_copy(src_ref=src, dst_ref=dst, send_sem=send, recv_sem=recv,
                                            device_id=to, device_id_type=MESH)

    barrier = pltpu.get_barrier_semaphore()
    for t in range(1, parts):
        pl.semaphore_signal(barrier, inc=1, device_id=across(t), device_id_type=MESH)
    for i in range(1, members):
        pl.semaphore_signal(barrier, inc=1, device_id=along(i), device_id_type=MESH)

    sums[0] = jnp.zeros((8, width), jnp.float32)

    @pl.loop(0, rows // 64)
    def _(r):
        block = x_ref[pl.ds(pl.multiple_of(r * 64, 64), 64), :].astype(jnp.float32)
        sums[0] += jnp.sum(block.reshape(8, 8, width), axis=0)

    pl.semaphore_wait(barrier, parts + members - 2)

    sent = []
    sum_copies = []
    for t in range(1, parts):
        copy = remote(sums.at[0], sums.at[t], sum_send.at[t], sum_recv.at[t], across(t))
        copy.start()
        sum_copies.append(copy)
    sent += sum_copies

    relay = parts == 4

    def raw_copy(t, h, src, to):
        at = pl.ds(h * half, half)
        return remote(src.at[at, :], raw.at[t, at, :], raw_send.at[t, h], raw_recv.at[t, h], to)

    raw_copies = {}
    for n in range(2):
        for t in range(1, 3 if relay else parts):
            h = (n + t - 1) % 2
            raw_copies[t, h] = raw_copy(t, h, x_ref, across(t))
            raw_copies[t, h].start()

    for copy in sum_copies:
        copy.wait_recv()
    total = sums[0]
    for t in range(1, parts):
        total = total + sums[t]
    mean = jnp.sum(total, axis=0, keepdims=True) / batch

    gram_copies = []

    def do_part(t):
        @pl.loop(0, rows // 64)
        def _(r):
            at = pl.ds(pl.multiple_of(r * 64, 64), 64)
            block = x_ref[at, :] if t == 0 else raw[t, at, :]
            cent[t, at, :] = (block.astype(jnp.float32) - mean).astype(jnp.bfloat16)

        for n in range(rows // 256):
            gram[t, :, n * 256:(n + 1) * 256] = lax.dot_general(
                cent[0], cent[t, n * 256:(n + 1) * 256, :], (((1,), (1,)), ((), ())),
                preferred_element_type=jnp.float32).astype(jnp.bfloat16)
        for i in range(1, members):
            to = lax.rem(me + i, members)
            copy = remote(gram.at[t, pl.ds(to * piece, piece), :], held.at[me, t],
                          gram_send.at[t, i], gram_recv.at[t, i], along(i))
            copy.start()
            gram_copies.append(copy)
        held[me, t] = gram[t, pl.ds(pl.multiple_of(me * piece, piece), piece), :]

    do_part(0)
    if relay:
        raw_copies[1, 0].wait_recv()
        raw_copies[3, 0] = raw_copy(3, 0, raw.at[1], across(2))
        raw_copies[3, 0].start()
        raw_copies[2, 1].wait_recv()
        raw_copies[3, 1] = raw_copy(3, 1, raw.at[2], across(1))
        raw_copies[3, 1].start()
        raw_copies[1, 1].wait_recv()
        do_part(1)
        raw_copies[2, 0].wait_recv()
        do_part(2)
        raw_copies[3, 0].wait_recv()
        raw_copies[3, 1].wait_recv()
        do_part(3)
    else:
        for t in range(1, parts):
            raw_copies[t, 0].wait_recv()
            raw_copies[t, 1].wait_recv()
            do_part(t)
    sent += list(raw_copies.values()) + gram_copies

    tall = min(piece, 32)
    chunks = [(a, b) for a in range(0, piece, tall) for b in range(0, rows, LANES)]
    per_row = rows // LANES
    acc[...] = jnp.zeros(acc.shape, jnp.float32)
    for t in range(parts):
        for i in range(1, members):
            remote(gram.at[t, pl.ds(0, piece), :], held.at[source(i), t], gram_send.at[t, i],
                   gram_recv.at[t, i], along(i)).wait_recv()

        @pl.loop(0, len(chunks))
        def _(c):
            down = pl.ds(pl.multiple_of((c // per_row) * tall, tall), tall)
            over = pl.ds(pl.multiple_of((c % per_row) * LANES, LANES), LANES)
            tiles = [held[q, t, down, over].astype(jnp.float32) for q in range(members)]
            for o in range(pairs + 1):
                for q in range(members):
                    product = tiles[q] * tiles[(q + o) % members]
                    acc[o, q] += jnp.sum(product.reshape(tall // 8, 8, LANES), axis=0)

    for o in range(pairs + 1):
        stage[0, o] = jnp.sum(acc[o], axis=1)
    small = []
    for t in range(1, parts):
        copy = remote(stage.at[0], stage.at[t], acc_send.at[t], acc_recv.at[t], across(t))
        copy.start()
        small.append(copy)
    for copy in small:
        copy.wait_recv()
    value = stage[0]
    for t in range(1, parts):
        value = value + stage[t]
    stage[parts] = value
    for i in range(1, members):
        copy = remote(stage.at[parts], stage.at[parts + i], acc_send.at[parts + i],
                      acc_recv.at[parts + i], along(i))
        copy.start()
        small.append(copy)
    for copy in small[parts - 1:]:
        copy.wait_recv()
    sent += small
    for i in range(1, members):
        value = value + stage[parts + i]
    hsic = [jnp.broadcast_to(jnp.sum(value[o], axis=1, keepdims=True), (members, LANES))
            for o in range(pairs + 1)]
    column = lax.broadcasted_iota(jnp.int32, (members, LANES), 1)
    row = lax.broadcasted_iota(jnp.int32, (members, LANES), 0)
    scores = jnp.zeros((members, LANES), jnp.float32)
    load = jnp.zeros((members, LANES), jnp.float32)
    for o in range(1, pairs + 1):
        norm = jnp.sqrt(hsic[0] * rolled(hsic[0], -o))
        cka = hsic[o] / norm
        scores = jnp.where(column == o - 1, cka, scores)
        weighted = weight_ref[o - 1] * cka
        load = load + weighted + rolled(weighted, o)
        coefs[o] = 2.0 * weight_ref[o - 1] / norm
    coefs[0] = -2.0 * (load / (hsic[0] + 1e-06))
    own = jnp.sum(jnp.where(row == me, scores, 0.0), axis=0, keepdims=True)
    cka_ref[...] = own[:, :pairs]

    back_copies = []
    for t in range(parts):
        @pl.loop(0, len(chunks))
        def _(c):
            down = pl.ds(pl.multiple_of((c // per_row) * tall, tall), tall)
            over = pl.ds(pl.multiple_of((c % per_row) * LANES, LANES), LANES)
            tiles = [held[q, t, down, over].astype(jnp.float32) for q in range(members)]
            for m in range(members):
                out = coefs[0, m:m + 1, :] * tiles[m]
                for o in range(1, pairs + 1):
                    p, q = (m + o) % members, (m - o) % members
                    out = out + coefs[o, m:m + 1, :] * tiles[p] + coefs[o, q:q + 1, :] * tiles[q]
                mixed[m, t, down, over] = out.astype(jnp.bfloat16)

        for i in range(1, members):
            to = lax.rem(me + i, members)
            copy = remote(mixed.at[to, t], back.at[t, pl.ds(me * piece, piece), :],
                          back_send.at[t, i], back_recv.at[t, i], along(i))
            copy.start()
            back_copies.append(copy)
        back[t, pl.ds(pl.multiple_of(me * piece, piece), piece), :] = mixed[me, t]
    sent += back_copies

    scale = math.sqrt(batch)
    for t in range(parts):
        for i in range(1, members):
            remote(mixed.at[0, t], back.at[t, pl.ds(source(i) * piece, piece), :],
                   back_send.at[t, i], back_recv.at[t, i], along(i)).wait_recv()

        @pl.loop(0, width // 256)
        def _(n):
            over = pl.ds(pl.multiple_of(n * 256, 256), 256)
            part = jnp.dot(back[t], cent[t, :, over], preferred_element_type=jnp.float32)
            if t > 0:
                part = grad_ref[:, over] + part
            if t == parts - 1:
                part = scale * part
            grad_ref[:, over] = part

    for copy in sent:
        copy.wait_send()


def shards(feats, pair_weight):
    rows = feats[0]
    parts, members = lax.axis_size("dp"), lax.axis_size("member")
    count, width = rows.shape
    pairs = pair_weight.shape[1]
    piece = count // members
    weights = jnp.broadcast_to(pair_weight.T[:, :, None], (pairs, members, LANES))
    dma = pltpu.SemaphoreType.DMA
    grad, cka = pl.pallas_call(
        functools.partial(kernel, members, parts, pairs),
        out_shape=(jax.ShapeDtypeStruct((count, width), jnp.float32),
                   jax.ShapeDtypeStruct((1, pairs), jnp.float32)),
        in_specs=[pl.BlockSpec(memory_space=pltpu.VMEM)] * 2,
        out_specs=(pl.BlockSpec(memory_space=pltpu.VMEM),) * 2,
        scratch_shapes=[
            pltpu.VMEM((parts, 8, width), jnp.float32),
            pltpu.VMEM((parts, count, width), jnp.bfloat16),
            pltpu.VMEM((parts, count, width), jnp.bfloat16),
            pltpu.VMEM((parts, count, count), jnp.bfloat16),
            pltpu.VMEM((members, parts, piece, count), jnp.bfloat16),
            pltpu.VMEM((members, parts, piece, count), jnp.bfloat16),
            pltpu.VMEM((parts, count, count), jnp.bfloat16),
            pltpu.VMEM((pairs + 1, members, 8, LANES), jnp.float32),
            pltpu.VMEM((parts + members, pairs + 1, members, LANES), jnp.float32),
            pltpu.VMEM((pairs + 1, members, LANES), jnp.float32),
            dma((parts,)), dma((parts,)),
            dma((parts, 2)), dma((parts, 2)),
            dma((parts, members)), dma((parts, members)),
            dma((parts, members)), dma((parts, members)),
            dma((parts + members,)), dma((parts + members,)),
        ],
        compiler_params=pltpu.CompilerParams(
            collective_id=0, has_side_effects=True, vmem_limit_bytes=60 * 1024 * 1024),
    )(rows, weights)
    return (grad[None], cka)


def solution(mesh):
    return jax.shard_map(
        shards,
        mesh=mesh,
        in_specs=(P("member", "dp", None), P()),
        out_specs=(P("member", "dp", None), P("member", None)),
        check_vma=False,
    )
```

time: 293 us -> 131 us (0.45)
  waiting for transfers between devices: 155 us -> 0 us
  Pallas kernels: 0 us -> 123 us
  other arithmetic: 58.2 us -> 0 us
  blocking collectives: 37 us -> 0 us
  between operations: 14.1 us -> 0.65 us
  matrix products: 9.6 us -> 0 us
  starting transfers between devices: 8.86 us -> 0 us
  local copies, waits for them, and re-layouts: 9.6 us -> 5.03 us
    pallas_call x0 -> x1, Pallas kernels: none -> 123 us  [shards(): pl.pallas_call(functools.partial(kernel, members, parts, pairs), out_shap...]
    all_to_all x2 -> x0, waiting for transfers between devices: 97 us -> none  [the longest x1 48.6 us: shards(): held = lax.all_to_all(gram.astype(jnp.bfloat16), 'member', 0, 0)]
    all_gather x1 -> x0, waiting for transfers between devices: 57.2 us -> none  [shards(): whole = lax.all_gather(rows, 'dp', axis=0, tiled=True)]
    unnamed x7 -> x0, other arithmetic: 43.5 us -> none
    psum x1 -> x0, blocking collectives: 37 us -> none  [shards(): sums = lax.psum(jnp.stack(sums, axis=1), ('member', 'dp'))]
    dot_general x2 -> x0, matrix products: 9.6 us -> none  [the longest x1 5.85 us: shards(): jnp.einsum('jrc,jcf->rf', mixed, blocks, preferred_element_type=jnp.float32)]
    all_to_all x2 -> x0, starting transfers between devices: 8.82 us -> none  [the longest x1 4.6 us: shards(): held = lax.all_to_all(gram.astype(jnp.bfloat16), 'member', 0, 0)]
    another operation x5 -> x0, other arithmetic: 7.11 us -> none  [the longest x1 6.23 us: shards(): jnp.stack([sum((mix[m, q] * held[q] for q in range(members))) for m in ra...]
  transfers between devices with their start and end apart: 3 -> 0, of which waited for: 3 -> 0; matrix products, arithmetic and copies ran while one was open for 0% -> 0% of each run, Pallas kernels for 0% -> 0%
where the time goes in v2:
time: 131 us; the launch traced here: 129 us
  Pallas kernels  123 us (94%)
  local copies, waits for them, and re-layouts  5.03 us (4%)
    pallas_call x1, Pallas kernels, shards(): pl.pallas_call(functools.partial(kernel, members, parts, pairs), out_shap...  123 us
    unnamed x4, local copies, waits for them, and re-layouts  3.67 us

profile of v2, /device:TPU:0, one launch (start us, length us, event | category | flops | bytes accessed | tf_op | source)
XLA Modules:
  0.0 128.7 jit_solution(10543368056405770817)
XLA Ops:
  0.6 1.4 %broadcast_in_dim.4.weight_ref = f32[3,8,128]{2,1,0:T(8,128)} broadcast(f32[3,8]{1,0:T(4,128)} %bitcast.5), dimensions={0,1} | broadcast | bytes 12384 | tf_op jit(solution)/shard_map/broadcast_in_dim | solution.py:248
  2.0 123.0 %shard_map.41 = (f32[512,1024]{1,0:T(8,128)}, f32[1,3]{1,0:T(1,128)}) custom-call(bf16[512,1024]{1,0:T(8,128)(2,1)} %bitcast.4, f32[3,8,128]{2,1,0:T(8,128)} %broadcast_in_dim.4.weight_ref), custom_call_target="tpu_custom_call" | custom-call | tf_op jit(solution)/shard_map/pallas_call | solution.py:250
  125.0 0.0 copy-start
  125.0 3.2 %copy.6 = f32[1,512,1024]{2,1,0:T(8,128)} copy(f32[1,512,1024]{2,1,0:T(8,128)} %bitcast.3) | data formatting | bytes 4194304
  128.1 0.0 copy-done
  128.1 0.5 copy.7
Async XLA Ops:
  125.0 3.2 %copy-start = (f32[1,3]{1,0:T(1,128)S(1)}, f32[1,3]{1,0:T(1,128)}, u32[]{:S(2)}) copy-start(f32[1,3]{1,0:T(1,128)} %get-tuple-element.9) | copy-start | bytes 40

commit v3 on v2

v3 whole, which is shorter than its diff:
```python
import functools
import math

import jax
import jax.numpy as jnp
from jax import lax
from jax.experimental import pallas as pl
from jax.experimental.pallas import tpu as pltpu
from jax.sharding import PartitionSpec as P

MESH = pl.DeviceIdType.MESH
LANES = 128


def ring(index, count):
    if count != 4:
        return index
    return 2 * (index // 2) + ((index % 2) + (index // 2)) % 2


def rolled(value, steps):
    count = value.shape[0]
    steps %= count
    if steps == 0:
        return value
    return jnp.concatenate([value[count - steps:], value[:count - steps]], axis=0)


def kernel(members, parts, pairs, x_ref, weight_ref, grad_ref, cka_ref, sums, raw, cent, gram, held,
           mixed, back, turned, acc, stage, coefs, sum_send, sum_recv, raw_send, raw_recv, gram_send,
           gram_recv, back_send, back_recv, pass_send, pass_recv, acc_send, acc_recv):
    me = lax.axis_index("member")
    place = ring(lax.axis_index("dp"), parts)
    rows, width = x_ref.shape
    piece = rows // members
    half = rows // 2
    batch = rows * parts
    opposite = parts // 2
    upper = place // opposite

    def across(t):
        return {"member": me, "dp": ring(lax.rem(place + t, parts), parts)}

    def along(i):
        return {"member": lax.rem(me + i, members), "dp": lax.axis_index("dp")}

    def source(i):
        return lax.rem(me + members - i, members)

    def remote(src, dst, send, recv, to):
        return pltpu.make_async_remote_copy(src_ref=src, dst_ref=dst, send_sem=send, recv_sem=recv,
                                            device_id=to, device_id_type=MESH)

    def depth(b):
        return piece // 2 if b == opposite else piece

    def slab(b):
        return pl.ds(b * piece, depth(b))

    barrier = pltpu.get_barrier_semaphore()
    for t in range(1, parts):
        pl.semaphore_signal(barrier, inc=1, device_id=across(t), device_id_type=MESH)
    for i in range(1, members):
        pl.semaphore_signal(barrier, inc=1, device_id=along(i), device_id_type=MESH)

    sums[0] = jnp.zeros((8, width), jnp.float32)

    @pl.loop(0, rows // 64)
    def _(r):
        block = x_ref[pl.ds(pl.multiple_of(r * 64, 64), 64), :].astype(jnp.float32)
        sums[0] += jnp.sum(block.reshape(8, 8, width), axis=0)

    pl.semaphore_wait(barrier, parts + members - 2)

    sent = []
    sum_copies = []
    for t in range(1, parts):
        copy = remote(sums.at[0], sums.at[parts - t], sum_send.at[t], sum_recv.at[parts - t], across(t))
        copy.start()
        sum_copies.append(copy)
    sent += sum_copies

    relay = parts == 4

    def send_raw(t, h, src, slot, to):
        at = pl.ds(h * half, half)
        copy = remote(src.at[at, :], raw.at[slot, at, :], raw_send.at[t, h], raw_recv.at[slot, h], to)
        copy.start()
        sent.append(copy)

    def wait_raw(slot, h):
        at = pl.ds(h * half, half)
        remote(x_ref.at[at, :], raw.at[slot, at, :], raw_send.at[slot, h], raw_recv.at[slot, h],
               across(slot)).wait_recv()

    if relay:
        send_raw(3, 0, x_ref, 1, across(3))
        send_raw(1, 1, x_ref, 3, across(1))
        send_raw(3, 1, x_ref, 1, across(3))
    else:
        for t in range(parts - 1, 0, -1):
            for h in range(2):
                send_raw(t, h, x_ref, parts - t, across(t))

    for copy in sum_copies:
        copy.wait_recv()
    total = sums[0]
    for t in range(1, parts):
        total = total + sums[t]
    mean = jnp.sum(total, axis=0, keepdims=True) / batch

    def centre(t):
        @pl.loop(0, rows // 64)
        def _(r):
            at = pl.ds(pl.multiple_of(r * 64, 64), 64)
            block = x_ref[at, :] if t == 0 else raw[t, at, :]
            cent[t, at, :] = (block.astype(jnp.float32) - mean).astype(jnp.bfloat16)

    def multiply(b):
        centre(b)
        if b == opposite:
            left = cent[upper * opposite, pl.ds(pl.multiple_of(upper * half, half), half), :]
        else:
            left = cent[0]
        other = (1 - upper) * opposite if b == opposite else b
        tall = left.shape[0]
        for n in range(rows // 256):
            gram[b, :tall, n * 256:(n + 1) * 256] = lax.dot_general(
                left, cent[other, n * 256:(n + 1) * 256, :], (((1,), (1,)), ((), ())),
                preferred_element_type=jnp.float32).astype(jnp.bfloat16)
        for i in range(1, members):
            to = lax.rem(me + i, members)
            copy = remote(gram.at[b, pl.ds(to * depth(b), depth(b)), :], held.at[me, slab(b)],
                          gram_send.at[b, i], gram_recv.at[b, i], along(i))
            copy.start()
            sent.append(copy)
        held[me, slab(b)] = gram[b, pl.ds(pl.multiple_of(me * depth(b), depth(b)), depth(b)), :]

    def chunks(b):
        tall = min(depth(b), 32)
        per_row = rows // LANES

        def place_of(c):
            down = pl.ds(pl.multiple_of(b * piece + (c // per_row) * tall, tall), tall)
            return down, pl.ds(pl.multiple_of((c % per_row) * LANES, LANES), LANES)

        return tall, (depth(b) // tall) * per_row, place_of

    def score(b):
        for i in range(1, members):
            remote(gram.at[b, pl.ds(0, depth(b)), :], held.at[source(i), slab(b)], gram_send.at[b, i],
                   gram_recv.at[b, i], along(i)).wait_recv()
        tall, count, place_of = chunks(b)

        @pl.loop(0, count)
        def _(c):
            down, over = place_of(c)
            tiles = [held[q, down, over].astype(jnp.float32) for q in range(members)]
            for o in range(pairs + 1):
                for q in range(members):
                    product = tiles[q] * tiles[(q + o) % members]
                    acc[o, q] += jnp.sum(product.reshape(tall // 8, 8, LANES), axis=0)

    multiply(0)
    if relay:
        wait_raw(1, 0)
        send_raw(2, 0, raw.at[1], 2, across(3))
        wait_raw(3, 1)
        send_raw(2, 1, raw.at[3], 2, across(1))
        send_raw(1, 0, x_ref, 3, across(1))
        wait_raw(1, 1)
    acc[...] = jnp.zeros(acc.shape, jnp.float32)
    for b in range(1, opposite + 1):
        if not relay or b == opposite:
            wait_raw(b, 0)
            wait_raw(b, 1)
        if b == opposite:
            score(0)
            acc[...] = 0.5 * acc[...]
        multiply(b)
    for t in range(opposite + 1, parts):
        if not relay:
            wait_raw(t, 1)
        wait_raw(t, 0)
        centre(t)
    for b in range(1, opposite + 1):
        score(b)

    for o in range(pairs + 1):
        stage[0, o] = 2.0 * jnp.sum(acc[o], axis=1)
    small = []
    for t in range(1, parts):
        copy = remote(stage.at[0], stage.at[parts - t], acc_send.at[t], acc_recv.at[parts - t], across(t))
        copy.start()
        small.append(copy)
    for copy in small:
        copy.wait_recv()
    value = stage[0]
    for t in range(1, parts):
        value = value + stage[t]
    stage[parts] = value
    for i in range(1, members):
        copy = remote(stage.at[parts], stage.at[parts + i], acc_send.at[parts + i],
                      acc_recv.at[parts + i], along(i))
        copy.start()
        small.append(copy)
    for copy in small[parts - 1:]:
        copy.wait_recv()
    sent += small
    everyone = [value] + [stage[parts + i] for i in range(1, members)]
    while len(everyone) > 1:
        everyone = [sum(everyone[n:n + 2]) for n in range(0, len(everyone), 2)]
    hsic = [jnp.broadcast_to(jnp.sum(everyone[0][o], axis=1, keepdims=True), (members, LANES))
            for o in range(pairs + 1)]
    column = lax.broadcasted_iota(jnp.int32, (members, LANES), 1)
    row = lax.broadcasted_iota(jnp.int32, (members, LANES), 0)
    scores = jnp.zeros((members, LANES), jnp.float32)
    load = jnp.zeros((members, LANES), jnp.float32)
    for o in range(1, pairs + 1):
        weight = jnp.broadcast_to(weight_ref[:, o - 1:o], (members, LANES))
        norm = jnp.sqrt(hsic[0] * rolled(hsic[0], -o))
        cka = hsic[o] / norm
        scores = jnp.where(column == o - 1, cka, scores)
        weighted = weight * cka
        load = load + weighted + rolled(weighted, o)
        coefs[o] = 2.0 * weight / norm
    coefs[0] = -2.0 * (load / (hsic[0] + 1e-06))
    own = jnp.sum(jnp.where(row == me, scores, 0.0), axis=0, keepdims=True)
    cka_ref[...] = own[:, :pairs]

    def landing(b, member):
        start = upper * half if b == opposite else 0
        return pl.ds(pl.multiple_of(start + member * depth(b), depth(b)), depth(b))

    def pass_on(b, i):
        if b == 0:
            return
        at = landing(b, source(i))
        copy = remote(back.at[b, at, :], back.at[parts - b, at, :], pass_send.at[b, i],
                      pass_recv.at[b, i], across(b))
        copy.start()
        sent.append(copy)

    def mix(b):
        tall, count, place_of = chunks(b)

        @pl.loop(0, count)
        def _(c):
            down, over = place_of(c)
            tiles = [held[q, down, over].astype(jnp.float32) for q in range(members)]
            for m in range(members):
                out = coefs[0, m:m + 1, :] * tiles[m]
                for o in range(1, pairs + 1):
                    p, q = (m + o) % members, (m - o) % members
                    out = out + coefs[o, m:m + 1, :] * tiles[p] + coefs[o, q:q + 1, :] * tiles[q]
                mixed[m, down, over] = out.astype(jnp.bfloat16)

        for i in range(1, members):
            to = lax.rem(me + i, members)
            copy = remote(mixed.at[to, slab(b)], back.at[b, landing(b, me), :],
                          back_send.at[b, i], back_recv.at[b, i], along(i))
            copy.start()
            sent.append(copy)
        back[b, landing(b, me), :] = mixed[me, slab(b)]
        pass_on(b, 0)

    order = list(range(1, opposite + 1)) + [0]
    for b in order:
        mix(b)

    scale = math.sqrt(batch)

    def add(left, t, first=False, last=False):
        @pl.loop(0, width // 256)
        def _(n):
            over = pl.ds(pl.multiple_of(n * 256, 256), 256)
            part = jnp.dot(left[...], cent[t, :, over], preferred_element_type=jnp.float32)
            if not first:
                part = grad_ref[:, over] + part
            if last:
                part = scale * part
            grad_ref[:, over] = part

    def turn(t):
        turned[...] = back[t].T

    for n, b in enumerate(order):
        for i in range(1, members):
            remote(mixed.at[0, slab(b)], back.at[b, landing(b, source(i)), :], back_send.at[b, i],
                   back_recv.at[b, i], along(i)).wait_recv()
            pass_on(b, i)
        if b != opposite:
            add(back.at[b], b, first=n == 0)
    for b in range(1, opposite + 1):
        far = b == opposite
        for i in range(members):
            start = (1 - upper) * half if far else 0
            at = pl.ds(pl.multiple_of(start + source(i) * depth(b), depth(b)), depth(b))
            remote(back.at[b, pl.ds(0, depth(b)), :], back.at[parts - b, at, :], pass_send.at[b, i],
                   pass_recv.at[b, i], across(b)).wait_recv()
        if far:
            @pl.when(upper == 1)
            def _():
                turn(b)

            @pl.when(upper == 0)
            def _():
                turned[...] = back[b]
        else:
            turn(parts - b)
        add(turned, parts - b, last=far)

    for copy in sent:
        copy.wait_send()


def shards(feats, pair_weight):
    rows = feats[0]
    parts, members = lax.axis_size("dp"), lax.axis_size("member")
    count, width = rows.shape
    pairs = pair_weight.shape[1]
    piece = count // members
    blocks = parts // 2 + 1
    tall = piece * (parts // 2) + piece // 2
    dma = pltpu.SemaphoreType.DMA
    grad, cka = pl.pallas_call(
        functools.partial(kernel, members, parts, pairs),
        out_shape=(jax.ShapeDtypeStruct((count, width), jnp.float32),
                   jax.ShapeDtypeStruct((1, pairs), jnp.float32)),
        in_specs=[pl.BlockSpec(memory_space=pltpu.VMEM)] * 2,
        out_specs=(pl.BlockSpec(memory_space=pltpu.VMEM),) * 2,
        scratch_shapes=[
            pltpu.VMEM((parts, 8, width), jnp.float32),
            pltpu.VMEM((parts, count, width), jnp.bfloat16),
            pltpu.VMEM((parts, count, width), jnp.bfloat16),
            pltpu.VMEM((blocks, count, count), jnp.bfloat16),
            pltpu.VMEM((members, tall, count), jnp.bfloat16),
            pltpu.VMEM((members, tall, count), jnp.bfloat16),
            pltpu.VMEM((parts, count, count), jnp.bfloat16),
            pltpu.VMEM((count, count), jnp.bfloat16),
            pltpu.VMEM((pairs + 1, members, 8, LANES), jnp.float32),
            pltpu.VMEM((parts + members, pairs + 1, members, LANES), jnp.float32),
            pltpu.VMEM((pairs + 1, members, LANES), jnp.float32),
            dma((parts,)), dma((parts,)),
            dma((parts, 2)), dma((parts, 2)),
            dma((blocks, members)), dma((blocks, members)),
            dma((blocks, members)), dma((blocks, members)),
            dma((blocks, members)), dma((blocks, members)),
            dma((parts + members,)), dma((parts + members,)),
        ],
        compiler_params=pltpu.CompilerParams(
            collective_id=0, has_side_effects=True, vmem_limit_bytes=60 * 1024 * 1024),
    )(rows, pair_weight)
    return (grad[None], cka)


def solution(mesh):
    return jax.shard_map(
        shards,
        mesh=mesh,
        in_specs=(P("member", "dp", None), P()),
        out_specs=(P("member", "dp", None), P("member", None)),
        check_vma=False,
    )
```

time: 131 us -> 101 us (0.77)
  Pallas kernels: 123 us -> 93.8 us
    pallas_call x1, Pallas kernels: 123 us -> 93.8 us  [shards(): pl.pallas_call(functools.partial(kernel, members, parts, pairs), out_shap...]
    broadcast_in_dim x1 -> x0, local copies, waits for them, and re-layouts: 1.35 us -> none  [shards(): jnp.broadcast_to(pair_weight.T[:, :, None], (pairs, members, LANES))]
    unnamed x4 -> x5, local copies, waits for them, and re-layouts: 3.67 us -> 5.02 us
where the time goes in v3:
time: 101 us; the launch traced here: 99.5 us
  Pallas kernels  93.8 us (93%)
  local copies, waits for them, and re-layouts  5.02 us (5%)
    pallas_call x1, Pallas kernels, shards(): pl.pallas_call(functools.partial(kernel, members, parts, pairs), out_shap...  93.8 us
    unnamed x5, local copies, waits for them, and re-layouts  5.02 us

profile of v3, /device:TPU:0, one launch (start us, length us, event | category | flops | bytes accessed | tf_op | source)
XLA Modules:
  0.0 99.5 jit_solution(15402155420275696963)
XLA Ops:
  0.6 1.3 %copy.4.weight_ref = f32[8,3]{1,0:T(8,128)} copy(f32[8,3]{0,1:T(4,128)} %param.3) | data formatting | bytes 192 | tf_op args[1]
  2.0 93.8 %shard_map.41 = (f32[512,1024]{1,0:T(8,128)}, f32[1,3]{1,0:T(1,128)}) custom-call(bf16[512,1024]{1,0:T(8,128)(2,1)} %bitcast.3, f32[8,3]{1,0:T(8,128)} %copy.4.weight_ref), custom_call_target="tpu_custom_call" | custom-call | tf_op jit(solution)/shard_map/pallas_call | solution.py:326
  95.8 0.0 copy-start
  95.8 3.2 %copy.7 = f32[1,512,1024]{2,1,0:T(8,128)} copy(f32[1,512,1024]{2,1,0:T(8,128)} %bitcast.2) | data formatting | bytes 4194304
  99.0 0.0 copy-done
  99.0 0.5 copy.8
Async XLA Ops:
  95.8 3.2 %copy-start = (f32[1,3]{1,0:T(1,128)S(1)}, f32[1,3]{1,0:T(1,128)}, u32[]{:S(2)}) copy-start(f32[1,3]{1,0:T(1,128)} %get-tuple-element.9) | copy-start | bytes 40

commit v4 on v3

--- a/solution.py
+++ b/solution.py
@@ -27,7 +27,7 @@
 
 
 def kernel(members, parts, pairs, x_ref, weight_ref, grad_ref, cka_ref, sums, raw, cent, gram, held,
-           mixed, back, turned, acc, stage, coefs, sum_send, sum_recv, raw_send, raw_recv, gram_send,
+           mixed, back, middle, turned, acc, stage, coefs, sum_send, sum_recv, raw_send, raw_recv, gram_send,
            gram_recv, back_send, back_recv, pass_send, pass_recv, acc_send, acc_recv):
     me = lax.axis_index("member")
     place = ring(lax.axis_index("dp"), parts)
@@ -97,6 +97,7 @@
         send_raw(3, 0, x_ref, 1, across(3))
         send_raw(1, 1, x_ref, 3, across(1))
         send_raw(3, 1, x_ref, 1, across(3))
+        send_raw(1, 0, x_ref, 3, across(1))
     else:
         for t in range(parts - 1, 0, -1):
             for h in range(2):
@@ -109,32 +110,35 @@
         total = total + sums[t]
     mean = jnp.sum(total, axis=0, keepdims=True) / batch
 
-    def centre(t):
-        @pl.loop(0, rows // 64)
+    def centre(t, h):
+        @pl.loop(0, half // 64)
         def _(r):
-            at = pl.ds(pl.multiple_of(r * 64, 64), 64)
+            at = pl.ds(pl.multiple_of(h * half + r * 64, 64), 64)
             block = x_ref[at, :] if t == 0 else raw[t, at, :]
             cent[t, at, :] = (block.astype(jnp.float32) - mean).astype(jnp.bfloat16)
 
-    def multiply(b):
-        centre(b)
+    turns = ((place + 1) // 2) % 2
+    low = 1 + 2 * turns if relay else upper * opposite
+    high = 3 - 2 * turns if relay else (1 - upper) * opposite
+
+    def multiply(b, n):
         if b == opposite:
-            left = cent[upper * opposite, pl.ds(pl.multiple_of(upper * half, half), half), :]
+            left = cent[low, pl.ds(pl.multiple_of(upper * half, half), half), :]
         else:
             left = cent[0]
-        other = (1 - upper) * opposite if b == opposite else b
+        other = high if b == opposite else b
         tall = left.shape[0]
-        for n in range(rows // 256):
-            gram[b, :tall, n * 256:(n + 1) * 256] = lax.dot_general(
-                left, cent[other, n * 256:(n + 1) * 256, :], (((1,), (1,)), ((), ())),
-                preferred_element_type=jnp.float32).astype(jnp.bfloat16)
+        over = pl.ds(n * half, half)
+        gram[b, :tall, over] = lax.dot_general(
+            left, cent[other, over, :], (((1,), (1,)), ((), ())),
+            preferred_element_type=jnp.float32).astype(jnp.bfloat16)
         for i in range(1, members):
             to = lax.rem(me + i, members)
-            copy = remote(gram.at[b, pl.ds(to * depth(b), depth(b)), :], held.at[me, slab(b)],
-                          gram_send.at[b, i], gram_recv.at[b, i], along(i))
+            copy = remote(gram.at[b, pl.ds(to * depth(b), depth(b)), over], held.at[me, slab(b), over],
+                          gram_send.at[b, n, i], gram_recv.at[b, n, i], along(i))
             copy.start()
             sent.append(copy)
-        held[me, slab(b)] = gram[b, pl.ds(pl.multiple_of(me * depth(b), depth(b)), depth(b)), :]
+        held[me, slab(b), over] = gram[b, pl.ds(pl.multiple_of(me * depth(b), depth(b)), depth(b)), over]
 
     def chunks(b):
         tall = min(depth(b), 32)
@@ -147,9 +151,11 @@
         return tall, (depth(b) // tall) * per_row, place_of
 
     def score(b):
-        for i in range(1, members):
-            remote(gram.at[b, pl.ds(0, depth(b)), :], held.at[source(i), slab(b)], gram_send.at[b, i],
-                   gram_recv.at[b, i], along(i)).wait_recv()
+        for n in range(2):
+            over = pl.ds(n * half, half)
+            for i in range(1, members):
+                remote(gram.at[b, pl.ds(0, depth(b)), over], held.at[source(i), slab(b), over],
+                       gram_send.at[b, n, i], gram_recv.at[b, n, i], along(i)).wait_recv()
         tall, count, place_of = chunks(b)
 
         @pl.loop(0, count)
@@ -161,28 +167,42 @@
                     product = tiles[q] * tiles[(q + o) % members]
                     acc[o, q] += jnp.sum(product.reshape(tall // 8, 8, LANES), axis=0)
 
-    multiply(0)
+    for h in range(2):
+        centre(0, h)
+    for h in range(2):
+        multiply(0, h)
+    acc[...] = jnp.zeros(acc.shape, jnp.float32)
     if relay:
         wait_raw(1, 0)
+        centre(1, 0)
+        multiply(1, 0)
+        wait_raw(3, 1)
+        centre(3, 1)
+        score(0)
+        acc[...] = 0.5 * acc[...]
+        wait_raw(1, 1)
+        centre(1, 1)
+        multiply(1, 1)
+        wait_raw(3, 0)
         send_raw(2, 0, raw.at[1], 2, across(3))
-        wait_raw(3, 1)
         send_raw(2, 1, raw.at[3], 2, across(1))
-        send_raw(1, 0, x_ref, 3, across(1))
-        wait_raw(1, 1)
-    acc[...] = jnp.zeros(acc.shape, jnp.float32)
-    for b in range(1, opposite + 1):
-        if not relay or b == opposite:
-            wait_raw(b, 0)
-            wait_raw(b, 1)
-        if b == opposite:
-            score(0)
-            acc[...] = 0.5 * acc[...]
-        multiply(b)
-    for t in range(opposite + 1, parts):
-        if not relay:
-            wait_raw(t, 1)
-        wait_raw(t, 0)
-        centre(t)
+        centre(3, 0)
+        multiply(2, 0)
+        multiply(2, 1)
+    else:
+        for b in range(1, opposite + 1):
+            for h in range(2):
+                wait_raw(b, h)
+                centre(b, h)
+            if b == opposite:
+                score(0)
+                acc[...] = 0.5 * acc[...]
+            multiply(b, 0)
+            multiply(b, 1)
+        for t in range(opposite + 1, parts):
+            for h in range(2):
+                wait_raw(t, h)
+                centre(t, h)
     for b in range(1, opposite + 1):
         score(b)
 
@@ -228,18 +248,23 @@
     own = jnp.sum(jnp.where(row == me, scores, 0.0), axis=0, keepdims=True)
     cka_ref[...] = own[:, :pairs]
 
-    def landing(b, member):
-        start = upper * half if b == opposite else 0
+    def landing(b, member, side=upper):
+        start = side * half if b == opposite else 0
         return pl.ds(pl.multiple_of(start + member * depth(b), depth(b)), depth(b))
+
+    def arrival(b):
+        return middle if relay and b == opposite else back.at[b]
 
     def pass_on(b, i):
         if b == 0:
             return
         at = landing(b, source(i))
-        copy = remote(back.at[b, at, :], back.at[parts - b, at, :], pass_send.at[b, i],
-                      pass_recv.at[b, i], across(b))
-        copy.start()
-        sent.append(copy)
+        for step in (1, 3) if relay and b == opposite else (b,):
+            lane = 3 if step == 3 else b
+            copy = remote(arrival(b).at[at, :], back.at[parts - b, at, :], pass_send.at[lane, i],
+                          pass_recv.at[lane, i], across(step))
+            copy.start()
+            sent.append(copy)
 
     def mix(b):
         tall, count, place_of = chunks(b)
@@ -257,16 +282,21 @@
 
         for i in range(1, members):
             to = lax.rem(me + i, members)
-            copy = remote(mixed.at[to, slab(b)], back.at[b, landing(b, me), :],
+            copy = remote(mixed.at[to, slab(b)], arrival(b).at[landing(b, me), :],
                           back_send.at[b, i], back_recv.at[b, i], along(i))
             copy.start()
             sent.append(copy)
-        back[b, landing(b, me), :] = mixed[me, slab(b)]
+        arrival(b)[landing(b, me), :] = mixed[me, slab(b)]
         pass_on(b, 0)
 
     order = list(range(1, opposite + 1)) + [0]
     for b in order:
         mix(b)
+
+    if relay:
+        for h in range(2):
+            wait_raw(2, h)
+            centre(2, h)
 
     scale = math.sqrt(batch)
 
@@ -286,18 +316,22 @@
 
     for n, b in enumerate(order):
         for i in range(1, members):
-            remote(mixed.at[0, slab(b)], back.at[b, landing(b, source(i)), :], back_send.at[b, i],
+            remote(mixed.at[0, slab(b)], arrival(b).at[landing(b, source(i)), :], back_send.at[b, i],
                    back_recv.at[b, i], along(i)).wait_recv()
             pass_on(b, i)
         if b != opposite:
             add(back.at[b], b, first=n == 0)
     for b in range(1, opposite + 1):
         far = b == opposite
-        for i in range(members):
-            start = (1 - upper) * half if far else 0
-            at = pl.ds(pl.multiple_of(start + source(i) * depth(b), depth(b)), depth(b))
-            remote(back.at[b, pl.ds(0, depth(b)), :], back.at[parts - b, at, :], pass_send.at[b, i],
-                   pass_recv.at[b, i], across(b)).wait_recv()
+        if relay and far:
+            sides = [(2, lax.rem(place + 3, 4) // 2), (3, lax.rem(place + 1, 4) // 2)]
+        else:
+            sides = [(b, 1 - upper)]
+        for lane, side in sides:
+            for i in range(members):
+                at = landing(b, source(i), side)
+                remote(back.at[0, pl.ds(0, depth(b)), :], back.at[parts - b, at, :], pass_send.at[lane, i],
+                       pass_recv.at[lane, i], across(b)).wait_recv()
         if far:
             @pl.when(upper == 1)
             def _():
@@ -338,14 +372,15 @@
             pltpu.VMEM((members, tall, count), jnp.bfloat16),
             pltpu.VMEM((parts, count, count), jnp.bfloat16),
             pltpu.VMEM((count, count), jnp.bfloat16),
+            pltpu.VMEM((count, count), jnp.bfloat16),
             pltpu.VMEM((pairs + 1, members, 8, LANES), jnp.float32),
             pltpu.VMEM((parts + members, pairs + 1, members, LANES), jnp.float32),
             pltpu.VMEM((pairs + 1, members, LANES), jnp.float32),
             dma((parts,)), dma((parts,)),
             dma((parts, 2)), dma((parts, 2)),
+            dma((blocks, 2, members)), dma((blocks, 2, members)),
             dma((blocks, members)), dma((blocks, members)),
-            dma((blocks, members)), dma((blocks, members)),
-            dma((blocks, members)), dma((blocks, members)),
+            dma((blocks + 1, members)), dma((blocks + 1, members)),
             dma((parts + members,)), dma((parts + members,)),
         ],
         compiler_params=pltpu.CompilerParams(

time: 101 us -> 95.9 us (0.950)
  Pallas kernels: 93.8 us -> 88.8 us
    pallas_call x1, Pallas kernels: 93.8 us -> 88.8 us  [shards(): pl.pallas_call(functools.partial(kernel, members, parts, pairs), out_shap...]
where the time goes in v4:
time: 95.9 us; the launch traced here: 94.5 us
  Pallas kernels  88.8 us (93%)
  local copies, waits for them, and re-layouts  5.02 us (5%)
    pallas_call x1, Pallas kernels, shards(): pl.pallas_call(functools.partial(kernel, members, parts, pairs), out_shap...  88.8 us
    unnamed x5, local copies, waits for them, and re-layouts  5.02 us

profile of v4, /device:TPU:0, one launch (start us, length us, event | category | flops | bytes accessed | tf_op | source)
XLA Modules:
  0.0 94.5 jit_solution(15004808624521762522)
XLA Ops:
  0.6 1.3 %copy.4.weight_ref = f32[8,3]{1,0:T(8,128)} copy(f32[8,3]{0,1:T(4,128)} %param.3) | data formatting | bytes 192 | tf_op args[1]
  2.0 88.8 %shard_map.41 = (f32[512,1024]{1,0:T(8,128)}, f32[1,3]{1,0:T(1,128)}) custom-call(bf16[512,1024]{1,0:T(8,128)(2,1)} %bitcast.3, f32[8,3]{1,0:T(8,128)} %copy.4.weight_ref), custom_call_target="tpu_custom_call" | custom-call | tf_op jit(solution)/shard_map/pallas_call | solution.py:360
  90.8 0.0 copy-start
  90.8 3.2 %copy.7 = f32[1,512,1024]{2,1,0:T(8,128)} copy(f32[1,512,1024]{2,1,0:T(8,128)} %bitcast.2) | data formatting | bytes 4194304
  94.0 0.0 copy-done
  94.0 0.5 copy.8
Async XLA Ops:
  90.8 3.2 %copy-start = (f32[1,3]{1,0:T(1,128)S(1)}, f32[1,3]{1,0:T(1,128)}, u32[]{:S(2)}) copy-start(f32[1,3]{1,0:T(1,128)} %get-tuple-element.9) | copy-start | bytes 40

commit v5 on v4

--- a/solution.py
+++ b/solution.py
@@ -63,12 +63,12 @@
     for i in range(1, members):
         pl.semaphore_signal(barrier, inc=1, device_id=along(i), device_id_type=MESH)
 
-    sums[0] = jnp.zeros((8, width), jnp.float32)
-
-    @pl.loop(0, rows // 64)
-    def _(r):
+    def gather_sum(r, carry):
         block = x_ref[pl.ds(pl.multiple_of(r * 64, 64), 64), :].astype(jnp.float32)
-        sums[0] += jnp.sum(block.reshape(8, 8, width), axis=0)
+        return carry + jnp.sum(block.reshape(8, 8, width), axis=0)
+
+    partial = lax.fori_loop(0, rows // 64, gather_sum, jnp.zeros((8, width), jnp.float32))
+    sums[0] = jnp.sum(partial, axis=0, keepdims=True)
 
     pl.semaphore_wait(barrier, parts + members - 2)
 
@@ -108,7 +108,7 @@
     total = sums[0]
     for t in range(1, parts):
         total = total + sums[t]
-    mean = jnp.sum(total, axis=0, keepdims=True) / batch
+    mean = total / batch
 
     def centre(t, h):
         @pl.loop(0, half // 64)
@@ -206,8 +206,12 @@
     for b in range(1, opposite + 1):
         score(b)
 
+    column = lax.broadcasted_iota(jnp.int32, (members, LANES), 1)
+    packed = jnp.zeros((members, LANES), jnp.float32)
     for o in range(pairs + 1):
-        stage[0, o] = 2.0 * jnp.sum(acc[o], axis=1)
+        lanes = jnp.sum(jnp.sum(acc[o], axis=1), axis=1, keepdims=True)
+        packed = jnp.where(column == o, 2.0 * lanes, packed)
+    stage[0] = packed
     small = []
     for t in range(1, parts):
         copy = remote(stage.at[0], stage.at[parts - t], acc_send.at[t], acc_recv.at[parts - t], across(t))
@@ -230,9 +234,7 @@
     everyone = [value] + [stage[parts + i] for i in range(1, members)]
     while len(everyone) > 1:
         everyone = [sum(everyone[n:n + 2]) for n in range(0, len(everyone), 2)]
-    hsic = [jnp.broadcast_to(jnp.sum(everyone[0][o], axis=1, keepdims=True), (members, LANES))
-            for o in range(pairs + 1)]
-    column = lax.broadcasted_iota(jnp.int32, (members, LANES), 1)
+    hsic = [jnp.broadcast_to(everyone[0][:, o:o + 1], (members, LANES)) for o in range(pairs + 1)]
     row = lax.broadcasted_iota(jnp.int32, (members, LANES), 0)
     scores = jnp.zeros((members, LANES), jnp.float32)
     load = jnp.zeros((members, LANES), jnp.float32)
@@ -314,13 +316,16 @@
     def turn(t):
         turned[...] = back[t].T
 
-    for n, b in enumerate(order):
+    def collect(b):
         for i in range(1, members):
             remote(mixed.at[0, slab(b)], arrival(b).at[landing(b, source(i)), :], back_send.at[b, i],
                    back_recv.at[b, i], along(i)).wait_recv()
             pass_on(b, i)
+
+    for b in order[:-1]:
+        collect(b)
         if b != opposite:
-            add(back.at[b], b, first=n == 0)
+            add(back.at[b], b, first=b == 1)
     for b in range(1, opposite + 1):
         far = b == opposite
         if relay and far:
@@ -342,7 +347,9 @@
                 turned[...] = back[b]
         else:
             turn(parts - b)
-        add(turned, parts - b, last=far)
+        add(turned, parts - b, first=parts == 2)
+    collect(0)
+    add(back.at[0], 0, last=True)
 
     for copy in sent:
         copy.wait_send()
@@ -364,7 +371,7 @@
         in_specs=[pl.BlockSpec(memory_space=pltpu.VMEM)] * 2,
         out_specs=(pl.BlockSpec(memory_space=pltpu.VMEM),) * 2,
         scratch_shapes=[
-            pltpu.VMEM((parts, 8, width), jnp.float32),
+            pltpu.VMEM((parts, 1, width), jnp.float32),
             pltpu.VMEM((parts, count, width), jnp.bfloat16),
             pltpu.VMEM((parts, count, width), jnp.bfloat16),
             pltpu.VMEM((blocks, count, count), jnp.bfloat16),
@@ -374,7 +381,7 @@
             pltpu.VMEM((count, count), jnp.bfloat16),
             pltpu.VMEM((count, count), jnp.bfloat16),
             pltpu.VMEM((pairs + 1, members, 8, LANES), jnp.float32),
-            pltpu.VMEM((parts + members, pairs + 1, members, LANES), jnp.float32),
+            pltpu.VMEM((parts + members, members, LANES), jnp.float32),
             pltpu.VMEM((pairs + 1, members, LANES), jnp.float32),
             dma((parts,)), dma((parts,)),
             dma((parts, 2)), dma((parts, 2)),

time: 95.9 us -> 92.6 us (0.966); the launches traced: 94.5 us -> 92.4 us
  Pallas kernels: 88.8 us -> 86.7 us
    pallas_call x1, Pallas kernels: 88.8 us -> 86.7 us  [shards(): pl.pallas_call(functools.partial(kernel, members, parts, pairs), out_shap...]
where the time goes in v5:
time: 92.6 us; the launch traced here: 92.4 us
  Pallas kernels  86.7 us (94%)
  local copies, waits for them, and re-layouts  5.02 us (5%)
    pallas_call x1, Pallas kernels, shards(): pl.pallas_call(functools.partial(kernel, members, parts, pairs), out_shap...  86.7 us
    unnamed x5, local copies, waits for them, and re-layouts  5.02 us

profile of v5, /device:TPU:0, one launch (start us, length us, event | category | flops | bytes accessed | tf_op | source)
XLA Modules:
  0.0 92.4 jit_solution(5407921260408767333)
XLA Ops:
  0.6 1.3 %copy.4.weight_ref = f32[8,3]{1,0:T(8,128)} copy(f32[8,3]{0,1:T(4,128)} %param.3) | data formatting | bytes 192 | tf_op args[1]
  2.0 86.7 %shard_map.41 = (f32[512,1024]{1,0:T(8,128)}, f32[1,3]{1,0:T(1,128)}) custom-call(bf16[512,1024]{1,0:T(8,128)(2,1)} %bitcast.3, f32[8,3]{1,0:T(8,128)} %copy.4.weight_ref), custom_call_target="tpu_custom_call" | custom-call | tf_op jit(solution)/shard_map/pallas_call | solution.py:367
  88.7 0.0 copy-start
  88.7 3.2 %copy.7 = f32[1,512,1024]{2,1,0:T(8,128)} copy(f32[1,512,1024]{2,1,0:T(8,128)} %bitcast.2) | data formatting | bytes 4194304
  91.9 0.0 copy-done
  91.9 0.5 copy.8
Async XLA Ops:
  88.7 3.2 %copy-start = (f32[1,3]{1,0:T(1,128)S(1)}, f32[1,3]{1,0:T(1,128)}, u32[]{:S(2)}) copy-start(f32[1,3]{1,0:T(1,128)} %get-tuple-element.9) | copy-start | bytes 40
